TPU v7x, 32 devices: a whole 2x2x4 slice. The times are simulated.
32 devices in a mesh: rows: 8 (over y, x, core), snaps: 4 (over z).
Axes of the slice: x: 2, y: 2, z: 4, core: 2. Of those that a mesh axis runs over, the one named last changes fastest.
Arguments:
- snapshots: float32 [2048, 3072], P('rows', 'snaps'), may hold values from -6 to 6
Outputs:
- updated: float32 [2048, 3072], P('rows', 'snaps')
- factor_rows: float32 [1152, 3072], P(None, 'snaps')
All inputs are finite; a program needn't handle non-finite values.
Results may differ from a plain program's by a relative error of at most 0.00013.
Values sent between devices are 32-bit elements; how exact they have to be, the bound alone decides.
A program may use at most 64 MiB of HBM per device.

v0:
```python
import jax
import jax.numpy as jnp
from jax import lax
from jax.sharding import PartitionSpec as P

PANEL = 384
PANELS = 3


def spread(shard, axis, root):
    mine = lax.axis_index(axis) == root
    return lax.psum(jnp.where(mine, shard, jnp.zeros_like(shard)), axis)


def mult(left, right):
    return jnp.dot(left, right, precision=lax.Precision.HIGHEST, preferred_element_type=jnp.float32)


def fetch_panel(section, column_piece, n_snaps):
    return spread(column_piece, "snaps", section % n_snaps)


def shards(snapshots):
    rows_dev, cols_dev = snapshots.shape
    panel_width = PANEL
    n_snaps = lax.axis_size("snaps")
    my_snap = lax.axis_index("snaps")
    local_blocks = cols_dev // panel_width
    row_count = rows_dev * lax.axis_size("rows")
    root_rows = jnp.sqrt(jnp.float32(row_count))
    col_ids = jnp.arange(cols_dev, dtype=jnp.int32)
    turn_cols = col_ids // panel_width * n_snaps + my_snap
    identity = jnp.eye(panel_width, dtype=jnp.float32)
    working = snapshots
    coeff_rows = []
    slot_first = 0
    pending = fetch_panel(0, working[:, slot_first : slot_first + panel_width], n_snaps)
    for section in range(PANELS):
        panel_now = pending
        slot_index = section // n_snaps
        gram_matrix, cross_sums = lax.psum(
            (mult(panel_now.T, panel_now), mult(panel_now.T, working)), "rows"
        )
        factor = jnp.linalg.cholesky(gram_matrix)
        inverse = lax.linalg.triangular_solve(factor, identity, left_side=True, lower=True)
        orthobasis = mult(panel_now, inverse.T)
        coeffs = mult(inverse, cross_sums)
        applied = jnp.where((turn_cols > section)[None, :], coeffs, jnp.float32(0.0))
        working = working - mult(orthobasis, applied)
        low_own = slot_index * panel_width
        is_owner = my_snap == section % n_snaps
        own_cols = jnp.where(
            is_owner, orthobasis * root_rows, working[:, low_own : low_own + panel_width]
        )
        working = working.at[:, low_own : low_own + panel_width].set(own_cols)
        if section + 1 < PANELS:
            next_slot = (section + 1) // n_snaps
            low = next_slot * panel_width
            pending = fetch_panel(section + 1, working[:, low : low + panel_width], n_snaps)
        diagonal = jnp.where(
            (turn_cols == section)[None, :], jnp.tile(factor.T, (1, local_blocks)), jnp.float32(0.0)
        )
        coeff_rows.append((applied + diagonal) / root_rows)
    return (working, jnp.concatenate(coeff_rows, axis=0))


def solution(mesh):
    placed = (P("rows", "snaps"),)
    return jax.shard_map(
        shards,
        mesh=mesh,
        in_specs=placed,
        out_specs=(P("rows", "snaps"), P(None, "snaps")),
        check_vma=False,
    )
```

profile of v0, /device:TPU:27, one launch (start us, length us, event | category | flops | bytes accessed | tf_op | source)
XLA Modules:
  0.0 693.4 jit_solution(14924972085822224887)
XLA Ops:
  9.1 36.5 %all-reduce.11.cloned.1.call-done = f32[256,384]{1,0:T(8,128)} async-done(((f32[256,384]{1,0:T(8,128)}), f32[256,384]{1,0:T(8,128)}) %all-reduce.11.cloned.1.call-update) | async-done | bytes 393232 | tf_op jit(solution)/shard_map/psum | solution.py:12
  45.6 2.8 fusion.82
  51.5 60.3 %all-reduce.21.cloned.1.call-done = (f32[384,384]{0,1:T(8,128)}, f32[384,768]{1,0:T(8,128)}) async-done(((f32[384,384]{0,1:T(8,128)}, f32[384,768]{1,0:T(8,128)}), (f32[384,384]{0,1:T(8,128)}, f32[384,768]{1,0:T(8,128)})) %all-reduce.21.cloned.1.call-update) | async-done | bytes 1769488 | tf_op jit(solution)/shard_map/psum | solution.py:41
  113.3 11.7 %cholesky.273 = f32[128,128]{1,0:T(8,128)S(1)} custom-call(f32[128,128]{1,0:T(8,128)S(1)} %cholesky.428), custom_call_target="Cholesky" | custom-call | tf_op jit(solution)/shard_map/jit(cholesky)/cholesky | solution.py:44
  125.1 9.8 %custom-call.23 = f32[1,128,128]{1,2,0:T(8,128)S(1)} custom-call(f32[1,128,128]{2,1,0:T(8,128)S(1)} %get-tuple-element.129), custom_call_target="InvertDiagBlocksLowerTriangular" | custom-call | tf_op jit(solution)/shard_map/jit(cholesky)/cholesky | solution.py:44
  135.5 11.7 %cholesky.292 = f32[128,128]{1,0:T(8,128)S(1)} custom-call(f32[128,128]{1,0:T(8,128)S(1)} %cholesky.432), custom_call_target="Cholesky" | custom-call | tf_op jit(solution)/shard_map/jit(cholesky)/cholesky | solution.py:44
  147.2 10.0 %custom-call.24 = f32[1,128,128]{1,2,0:T(8,128)S(1)} custom-call(f32[1,128,128]{2,1,0:T(8,128)S(1)} %get-tuple-element.126), custom_call_target="InvertDiagBlocksLowerTriangular" | custom-call | tf_op jit(solution)/shard_map/jit(cholesky)/cholesky | solution.py:44
  157.7 11.7 %cholesky.311 = f32[128,128]{1,0:T(8,128)S(1)} custom-call(f32[128,128]{1,0:T(8,128)S(1)} %convolution_subtract_fusion.14), custom_call_target="Cholesky" | custom-call | tf_op jit(solution)/shard_map/jit(cholesky)/cholesky | solution.py:44
  172.9 6.0 while.9
  179.7 29.9 %custom-call.25 = f32[3,128,128]{1,2,0:T(8,128)S(1)} custom-call(f32[3,128,128]{2,1,0:T(8,128)S(1)} %get-tuple-element.60), custom_call_target="InvertDiagBlocksLowerTriangular" | custom-call | tf_op jit(solution)/shard_map/triangular_solve/custom-call.2 | solution.py:45
  221.1 34.9 %all-reduce.13.cloned.1.call-done = f32[256,384]{1,0:T(8,128)} async-done(((f32[256,384]{1,0:T(8,128)}), f32[256,384]{1,0:T(8,128)}) %all-reduce.13.cloned.1.call-update) | async-done | bytes 393232 | tf_op jit(solution)/shard_map/psum | solution.py:12
  256.0 2.8 fusion.84
  261.2 61.0 %all-reduce.19.cloned.1.call-done = (f32[384,384]{0,1:T(8,128)}, f32[384,768]{1,0:T(8,128)}) async-done(((f32[384,384]{0,1:T(8,128)}, f32[384,768]{1,0:T(8,128)}), (f32[384,384]{0,1:T(8,128)}, f32[384,768]{1,0:T(8,128)})) %all-reduce.19.cloned.1.call-update) | async-done | bytes 1769488 | tf_op jit(solution)/shard_map/psum | solution.py:41
  326.5 11.7 %cholesky.326 = f32[128,128]{1,0:T(8,128)S(1)} custom-call(f32[128,128]{1,0:T(8,128)S(1)} %cholesky.436), custom_call_target="Cholesky" | custom-call | tf_op jit(solution)/shard_map/jit(cholesky)/cholesky | solution.py:44
  339.1 9.8 %custom-call.26 = f32[1,128,128]{1,2,0:T(8,128)S(1)} custom-call(f32[1,128,128]{2,1,0:T(8,128)S(1)} %get-tuple-element.122), custom_call_target="InvertDiagBlocksLowerTriangular" | custom-call | tf_op jit(solution)/shard_map/jit(cholesky)/cholesky | solution.py:44
  351.9 11.7 %cholesky.345 = f32[128,128]{1,0:T(8,128)S(1)} custom-call(f32[128,128]{1,0:T(8,128)S(1)} %cholesky.440), custom_call_target="Cholesky" | custom-call | tf_op jit(solution)/shard_map/jit(cholesky)/cholesky | solution.py:44
  364.3 10.2 %custom-call.27 = f32[1,128,128]{1,2,0:T(8,128)S(1)} custom-call(f32[1,128,128]{2,1,0:T(8,128)S(1)} %get-tuple-element.119), custom_call_target="InvertDiagBlocksLowerTriangular" | custom-call | tf_op jit(solution)/shard_map/jit(cholesky)/cholesky | solution.py:44
  376.5 11.7 %cholesky.364 = f32[128,128]{1,0:T(8,128)S(1)} custom-call(f32[128,128]{1,0:T(8,128)S(1)} %convolution_subtract_fusion.13), custom_call_target="Cholesky" | custom-call | tf_op jit(solution)/shard_map/jit(cholesky)/cholesky | solution.py:44
  394.9 8.7 %while.10 = (s32[]{:T(128)}, f32[384,384]{1,0:T(8,128)}, s32[3,2]{0,1:T(2,128)S(1)}, f32[3,128,128]{2,1,0:T(8,128)S(1)}, s32[]{:T(128)}) while((s32[]{:T(128)}, f32[384,384]{1,0:T(8,128)}, s32[3,2]{0,1:T(2,128)S(1)}, f32[3,128,128]{2,1,0:T(8,128)S(1)}, s32[]{:T(128)}) %tuple.117), condition=%wide.while_cond.3.clone, body=%wide.while_body.3.clone.sunk | while | flops 2 | bytes 131189 | solution.py:45
  403.6 29.5 %custom-call.28 = f32[3,128,128]{1,2,0:T(8,128)S(1)} custom-call(f32[3,128,128]{2,1,0:T(8,128)S(1)} %get-tuple-element.61), custom_call_target="InvertDiagBlocksLowerTriangular" | custom-call | tf_op jit(solution)/shard_map/triangular_solve/custom-call.2 | solution.py:45
  442.4 3.1 add_multiply_fusion.1
  449.7 34.7 %all-reduce.15.cloned.1.call-done = f32[256,384]{1,0:T(8,128)} async-done(((f32[256,384]{1,0:T(8,128)}), f32[256,384]{1,0:T(8,128)}) %all-reduce.15.cloned.1.call-update) | async-done | bytes 393232 | tf_op jit(solution)/shard_map/psum | solution.py:12
  484.3 2.8 fusion.86
  489.4 61.2 %all-reduce.17.cloned.1.call-done = (f32[384,384]{0,1:T(8,128)}, f32[384,768]{1,0:T(8,128)}) async-done(((f32[384,384]{0,1:T(8,128)}, f32[384,768]{1,0:T(8,128)}), (f32[384,384]{0,1:T(8,128)}, f32[384,768]{1,0:T(8,128)})) %all-reduce.17.cloned.1.call-update) | async-done | bytes 1769488 | tf_op jit(solution)/shard_map/psum | solution.py:41
  554.8 11.7 %cholesky.379 = f32[128,128]{1,0:T(8,128)S(1)} custom-call(f32[128,128]{1,0:T(8,128)S(1)} %cholesky.444), custom_call_target="Cholesky" | custom-call | tf_op jit(solution)/shard_map/jit(cholesky)/cholesky | solution.py:44
  568.6 11.3 %custom-call.29 = f32[1,128,128]{1,2,0:T(8,128)} custom-call(f32[1,128,128]{2,1,0:T(8,128)} %get-tuple-element.115), custom_call_target="InvertDiagBlocksLowerTriangular" | custom-call | tf_op jit(solution)/shard_map/jit(cholesky)/cholesky | solution.py:44
  583.5 13.3 %cholesky.398 = f32[128,128]{1,0:T(8,128)} custom-call(f32[128,128]{1,0:T(8,128)} %cholesky.448), custom_call_target="Cholesky" | custom-call | tf_op jit(solution)/shard_map/jit(cholesky)/cholesky | solution.py:44
  598.8 11.3 %custom-call.30 = f32[1,128,128]{1,2,0:T(8,128)} custom-call(f32[1,128,128]{2,1,0:T(8,128)} %get-tuple-element.112), custom_call_target="InvertDiagBlocksLowerTriangular" | custom-call | tf_op jit(solution)/shard_map/jit(cholesky)/cholesky | solution.py:44
  612.9 13.2 %cholesky.417 = f32[128,128]{1,0:T(8,128)} custom-call(f32[128,128]{1,0:T(8,128)} %convolution_subtract_fusion.12), custom_call_target="Cholesky" | custom-call | tf_op jit(solution)/shard_map/jit(cholesky)/cholesky | solution.py:44
  632.6 8.8 %while.11 = (s32[]{:T(128)}, f32[384,384]{1,0:T(8,128)}, s32[3,2]{0,1:T(2,128)S(1)}, f32[3,128,128]{2,1,0:T(8,128)S(1)}, s32[]{:T(128)}) while((s32[]{:T(128)}, f32[384,384]{1,0:T(8,128)}, s32[3,2]{0,1:T(2,128)S(1)}, f32[3,128,128]{2,1,0:T(8,128)S(1)}, s32[]{:T(128)}) %tuple.118), condition=%wide.while_cond.3.clone.1, body=%wide.while_body.3.clone.1.sunk | while | flops 2 | bytes 131189 | solution.py:45
  633.5 2.2 bitcast_dynamic-update-slice_fusion.8
  641.5 29.5 %custom-call.31 = f32[3,128,128]{1,2,0:T(8,128)S(1)} custom-call(f32[3,128,128]{2,1,0:T(8,128)S(1)} %get-tuple-element.62), custom_call_target="InvertDiagBlocksLowerTriangular" | custom-call | tf_op jit(solution)/shard_map/triangular_solve/custom-call.2 | solution.py:45
  (171 shorter events, 110.2 us)
Async XLA Ops:
  7.2 38.5 %all-reduce.11.cloned.1.call-start = ((), (), s32[]{:S(2)}) async-start(), calls=%async_computation | async-start | bytes 786432 | tf_op jit(solution)/shard_map/psum | solution.py:12
  7.2 41.2 %copy-start.3 = (f32[256,768]{1,0:T(8,128)S(1)}, f32[256,768]{1,0:T(8,128)}, u32[]{:S(2)}) copy-start(f32[256,768]{1,0:T(8,128)} %param.10) | copy-start | bytes 2359300
  9.1 102.8 %all-reduce.21.cloned.1.call-start = ((), (), s32[]{:S(2)}) async-start(), calls=%async_computation.5 | async-start | bytes 3538944 | tf_op jit(solution)/shard_map/psum | solution.py:41
  45.6 2.8 copy-start
  50.6 205.4 %all-reduce.13.cloned.1.call-start = ((), (), s32[]{:S(2)}) async-start(), calls=%async_computation.1 | async-start | bytes 786432 | tf_op jit(solution)/shard_map/psum | solution.py:12
  111.8 1.4 copy-start.5
  178.9 0.8 copy-start.7
  213.8 1.3 copy-start.11
  221.1 101.1 %all-reduce.19.cloned.1.call-start = ((), (), s32[]{:S(2)}) async-start(), calls=%async_computation.4 | async-start | bytes 3538944 | tf_op jit(solution)/shard_map/psum | solution.py:41
  256.0 2.8 copy-start.1
  261.0 223.4 %all-reduce.15.cloned.1.call-start = ((), (), s32[]{:S(2)}) async-start(), calls=%async_computation.2 | async-start | bytes 786432 | tf_op jit(solution)/shard_map/psum | solution.py:12
  325.6 0.8 copy-start.9
  433.1 1.9 copy-start.17
  441.2 1.3 copy-start.12
  449.4 101.2 %all-reduce.17.cloned.1.call-start = ((), (), s32[]{:S(2)}) async-start(), calls=%async_computation.3 | async-start | bytes 3538944 | tf_op jit(solution)/shard_map/psum | solution.py:41
  484.3 2.8 copy-start.2
  550.6 2.2 copy-start.6
  553.9 0.8 copy-start.10
  566.5 0.6 copy-start.15
  582.2 0.7 copy-start.14
  671.0 1.9 copy-start.16
  677.1 1.3 copy-start.13
  683.0 1.3 copy-start.4
  683.7 2.5 copy-start.8
Sparse Core Ops, SparseCore 0:
  10.9 34.6 all-reduce.10
  50.7 61.0 all-reduce.20
  221.2 34.7 all-reduce.12
  261.1 61.0 all-reduce.18
  449.6 34.7 all-reduce.14
  489.5 61.0 all-reduce.16
where the time goes:
time: 701 us; the launch traced here: 693 us
  waiting for transfers between devices  289 us (41%)
  other arithmetic  285 us (41%)
  matrix products  53.1 us (8%)
  local copies, waits for them, and re-layouts  45.1 us (6%)
  between operations  20.7 us (3%)
    psum x3, waiting for transfers between devices, shards(): lax.psum((mult(panel_now.T, panel_now), mult(panel_now.T, working)), 'rows')  183 us
    another operation x32, other arithmetic, shards(): factor = jnp.linalg.cholesky(gram_matrix)  182 us
    psum x3, waiting for transfers between devices, spread(): return lax.psum(jnp.where(mine, shard, jnp.zeros_like(shard)), axis)  106 us
    another operation x4, other arithmetic, shards(): lax.linalg.triangular_solve(factor, identity, left_side=True, lower=True)  88.9 us
    dot_general x15, matrix products, mult(): jnp.dot(left, right, precision=lax.Precision.HIGHEST, preferred_element_t...  29.4 us
    another operation x31, local copies, waits for them, and re-layouts, shards(): lax.linalg.triangular_solve(factor, identity, left_side=True, lower=True)  23.1 us
  transfers between devices with their start and end apart: 6, of which 6 were waited for; matrix products, arithmetic and copies ran while one was open for 0% of the time, Pallas kernels for 0%

commit v1 on v0

v1 whole, which is shorter than its diff:
```python
import functools

import jax
import jax.numpy as jnp
from jax import lax
from jax.experimental import pallas as pl
from jax.experimental.pallas import tpu as pltpu
from jax.sharding import PartitionSpec as P

PANEL = 384
PANELS = 3
F32 = jnp.float32
BF16 = jnp.bfloat16


def dims(ta, tb):
    return (((0 if ta else 1,), (1 if tb else 0,)), ((), ()))


def dot6(a, b, ta=False, tb=False):
    return lax.dot_general(
        a, b, dims(ta, tb), precision=lax.Precision.HIGHEST, preferred_element_type=F32
    )


def dot1(a, b, ta=False, tb=False):
    return lax.dot_general(
        a.astype(BF16), b.astype(BF16), dims(ta, tb), preferred_element_type=F32
    )


def dot3(a, b, ta=False, tb=False):
    a_hi, b_hi = a.astype(BF16), b.astype(BF16)
    a_lo = (a - a_hi.astype(F32)).astype(BF16)
    b_lo = (b - b_hi.astype(F32)).astype(BF16)
    d = dims(ta, tb)
    return (
        lax.dot_general(a_hi, b_lo, d, preferred_element_type=F32)
        + lax.dot_general(a_lo, b_hi, d, preferred_element_type=F32)
        + lax.dot_general(a_hi, b_hi, d, preferred_element_type=F32)
    )


def grid_ids(n):
    return (
        lax.broadcasted_iota(jnp.int32, (n, n), 0),
        lax.broadcasted_iota(jnp.int32, (n, n), 1),
    )


def direct_inverse(x_ref, a_ref):
    n = a_ref.shape[0]
    row_ids, col_ids = grid_ids(n)
    x_ref[...] = jnp.where(row_ids == col_ids, F32(1), F32(0))

    @pl.loop(0, n)
    def _(j):
        a = a_ref[...]
        a_row = jnp.sum(jnp.where(row_ids == j, a, F32(0)), axis=0, keepdims=True)
        x = x_ref[...]
        x_row = jnp.sum(jnp.where(row_ids == j, x, F32(0)), axis=0, keepdims=True)
        a_col = jnp.sum(jnp.where(col_ids == j, a, F32(0)), axis=1, keepdims=True)
        pivot = jnp.sum(jnp.where(col_ids[:1] == j, a_row, F32(0)), axis=1, keepdims=True)
        ratio = jnp.where(row_ids[:, :1] > j, a_col / pivot, F32(0))
        a_ref[...] = a - ratio * a_row
        x_ref[...] = jnp.where(row_ids == j, x / jnp.sqrt(pivot), x - ratio * x_row)


def newton_inverse(x_ref, a_ref):
    n = a_ref.shape[0]
    row_ids, col_ids = grid_ids(n)
    on_diag = row_ids == col_ids
    a = a_ref[...]
    diag = jnp.sum(jnp.where(on_diag, a, F32(0)), axis=1, keepdims=True)
    x_ref[...] = jnp.where(on_diag, lax.rsqrt(diag), F32(0))

    def step(dot):
        x = x_ref[...]
        err = dot(dot(x, a_ref[...]), x, tb=True) - jnp.where(on_diag, F32(1), F32(0))
        half = jnp.where(row_ids > col_ids, err, jnp.where(on_diag, F32(0.5) * err, F32(0)))
        x_ref[...] = x - dot(half, x)
        return jnp.sum(err * err)

    def rough(state):
        count, size = state
        return count + 1, step(dot1)

    def fine(state):
        count, size = state
        return count + 1, step(dot6)

    count, size = lax.while_loop(
        lambda s: (s[0] < 12) & (s[1] > F32(0.5)), rough, (jnp.int32(0), F32(1e9))
    )
    count, size = lax.while_loop(
        lambda s: (s[0] < 24) & (s[1] > F32(1e-6)), fine, (count, F32(1e9))
    )

    @pl.when(jnp.logical_not(size <= F32(1e-6)))
    def _():
        direct_inverse(x_ref, a_ref)


def factor_kernel(root_rows, p_ref, w_ref, m_ref, g_ref, out_ref, fac_ref, q_ref, u_ref, c_ref, t_ref, x_ref):
    snap = lax.axis_index("snaps")
    n = PANEL
    row_ids, col_ids = grid_ids(n)
    width = w_ref.shape[1]
    chunks = [(c, n) for c in range(0, width, n)]

    def blk(k):
        return slice(k * n, (k + 1) * n)

    for k in range(PANELS):
        acc = m_ref[blk(k), blk(k)]
        for j in range(k):
            acc = acc - dot6(u_ref[blk(j), blk(k)], u_ref[blk(j), blk(k)], ta=True)
        t_ref[...] = acc
        newton_inverse(x_ref, t_ref)
        x = x_ref[...]
        for i in range(k + 1, PANELS):
            acc = m_ref[blk(k), blk(i)]
            for j in range(k):
                acc = acc - dot6(u_ref[blk(j), blk(k)], u_ref[blk(j), blk(i)], ta=True)
            u_ref[blk(k), blk(i)] = dot6(x, acc)
        for low, size in chunks:
            cols = slice(low, low + size)
            acc = g_ref[blk(k), cols]
            for j in range(k):
                acc = acc - dot3(u_ref[blk(j), blk(k)], c_ref[blk(j), cols], ta=True)
            coeffs = dot3(x, acc)
            if low == 0:
                keep = (snap > k) | ((snap == k) & (row_ids <= col_ids))
                coeffs = jnp.where(keep, coeffs, F32(0))
            c_ref[blk(k), cols] = coeffs
            fac_ref[blk(k), cols] = coeffs / root_rows
        rest = p_ref[:, blk(k)]
        for j in range(k):
            rest = rest - dot3(q_ref[:, blk(j)], u_ref[blk(j), blk(k)])
        q_ref[:, blk(k)] = dot3(rest, x, tb=True)

    for low, size in chunks:
        cols = slice(low, low + size)
        acc = w_ref[:, cols]
        for k in range(PANELS):
            acc = acc - dot3(q_ref[:, blk(k)], c_ref[blk(k), cols])
        out_ref[:, cols] = acc
    for k in range(PANELS):

        @pl.when(snap == k)
        def _():
            out_ref[:, :n] = q_ref[:, blk(k)] * root_rows


def shards(snapshots):
    rows_dev, cols_dev = snapshots.shape
    row_count = rows_dev * lax.axis_size("rows")
    root_rows = float(row_count) ** 0.5
    total = PANEL * PANELS
    panels = lax.all_gather(snapshots[:, :PANEL], "snaps", axis=1, tiled=True)[:, :total]
    gram, cross = lax.psum(
        (dot6(panels, panels, ta=True), dot6(panels, snapshots, ta=True)), "rows"
    )
    vmem = pl.BlockSpec(memory_space=pltpu.VMEM)
    return pl.pallas_call(
        functools.partial(factor_kernel, root_rows),
        out_shape=(
            jax.ShapeDtypeStruct((rows_dev, cols_dev), F32),
            jax.ShapeDtypeStruct((total, cols_dev), F32),
        ),
        in_specs=[vmem] * 4,
        out_specs=(vmem, vmem),
        scratch_shapes=[
            pltpu.VMEM((rows_dev, total), F32),
            pltpu.VMEM((total, total), F32),
            pltpu.VMEM((total, cols_dev), F32),
            pltpu.VMEM((PANEL, PANEL), F32),
            pltpu.VMEM((PANEL, PANEL), F32),
        ],
        compiler_params=pltpu.CompilerParams(vmem_limit_bytes=56 * 2**20),
    )(panels, snapshots, gram, cross)


def solution(mesh):
    assert mesh.shape["snaps"] >= PANELS
    return jax.shard_map(
        shards,
        mesh=mesh,
        in_specs=(P("rows", "snaps"),),
        out_specs=(P("rows", "snaps"), P(None, "snaps")),
        check_vma=False,
    )
```

time: 701 us -> 443 us (0.63)
  other arithmetic: 285 us -> 0 us
  Pallas kernels: 0 us -> 235 us
  waiting for transfers between devices: 289 us -> 169 us
  local copies, waits for them, and re-layouts: 45.1 us -> 2.95 us
  matrix products: 53.1 us -> 13.3 us
    another operation x37 -> x0, other arithmetic: 271 us -> none  [the longest x32 182 us: shards(): factor = jnp.linalg.cholesky(gram_matrix)]
    pallas_call x0 -> x1, Pallas kernels: none -> 235 us  [shards(): pl.pallas_call(functools.partial(factor_kernel, root_rows), out_shape=(ja...]
    psum x6 -> x1, waiting for transfers between devices: 289 us -> 132 us  [shards(): lax.psum((dot6(panels, panels, ta=True), dot6(panels, snapshots, ta=True)...]
    all_gather x0 -> x1, waiting for transfers between devices: none -> 37.1 us  [shards(): lax.all_gather(snapshots[:, :PANEL], 'snaps', axis=1, tiled=True)[:, :total]]
    another operation x43 -> x0, local copies, waits for them, and re-layouts: 27.8 us -> none  [the longest x31 23.1 us: shards(): lax.linalg.triangular_solve(factor, identity, left_side=True, lower=True)]
    another operation x27 -> x0, matrix products: 23.6 us -> none  [the longest x15 12.4 us: shards(): lax.linalg.triangular_solve(factor, identity, left_side=True, lower=True)]
    dot_general x15 -> x2, matrix products: 29.4 us -> 13.3 us  [dot6(): lax.dot_general(a, b, dims(ta, tb), precision=lax.Precision.HIGHEST, pref...]
    unnamed x39 -> x4, local copies, waits for them, and re-layouts: 7.98 us -> 0.01 us
  transfers between devices with their start and end apart: 6 -> 2, of which waited for: 6 -> 2; matrix products, arithmetic and copies ran while one was open for 0% -> 0% of each run, Pallas kernels for 0% -> 0%
where the time goes in v1:
time: 443 us; the launch traced here: 434 us
  Pallas kernels  235 us (53%)
  waiting for transfers between devices  169 us (38%)
  between operations  14.5 us (3%)
  matrix products  13.3 us (3%)
    pallas_call x1, Pallas kernels, shards(): pl.pallas_call(functools.partial(factor_kernel, root_rows), out_shape=(ja...  235 us
    psum x1, waiting for transfers between devices, shards(): lax.psum((dot6(panels, panels, ta=True), dot6(panels, snapshots, ta=True)...  132 us
    all_gather x1, waiting for transfers between devices, shards(): lax.all_gather(snapshots[:, :PANEL], 'snaps', axis=1, tiled=True)[:, :total]  37.1 us
    dot_general x2, matrix products, dot6(): lax.dot_general(a, b, dims(ta, tb), precision=lax.Precision.HIGHEST, pref...  13.3 us
  transfers between devices with their start and end apart: 2, of which 2 were waited for; matrix products, arithmetic and copies ran while one was open for 0% of the time, Pallas kernels for 0%

profile of v1, /device:TPU:27, one launch (start us, length us, event | category | flops | bytes accessed | tf_op | source)
XLA Modules:
  0.0 434.2 jit_solution(8149668616436368509)
XLA Ops:
  7.2 0.0 copy-start.1
  7.2 0.0 all-gather.2.cloned.1.call-start
  7.2 1.8 slice.6
  9.1 0.0 all-gather.2.cloned.1.call-update
  9.1 0.0 all-reduce.3.cloned.1.call-start
  9.1 37.1 %all-gather.2.cloned.1.call-done = f32[256,1536]{1,0:T(8,128)} async-done(((f32[256,384]{1,0:T(8,128)}), f32[256,1536]{1,0:T(8,128)}) %all-gather.2.cloned.1.call-update) | async-done | bytes 1572880 | tf_op jit(solution)/shard_map/all_gather | solution.py:160
  46.2 0.0 copy-done.1
  46.2 0.0 copy-start
  46.2 6.2 %fusion = f32[1152,768]{1,0:T(8,128)} fusion(f32[256,768]{1,0:T(8,128)S(1)} %copy-done.1, f32[256,1536]{1,0:T(8,128)} %all-gather.2.cloned.1.call-done), kind=kOutput, calls=%fused_computation | convolution fusion | flops 2717908992 | bytes 5505024 | tf_op jit(solution)/shard_map/dot_general | solution.py:21
  52.4 0.0 copy-done
  52.4 7.2 %fusion.2 = f32[1152,1152]{1,0:T(8,128)} fusion(f32[256,1536]{1,0:T(8,128)S(1)} %copy-done), kind=kOutput, calls=%fused_computation.2 | convolution fusion | flops 4076863488 | bytes 6488064 | tf_op jit(solution)/shard_map/dot_general | solution.py:21
  59.5 0.0 all-reduce.3.cloned.1.call-update
  59.6 1.1 slice.8.p_ref
  60.7 131.6 %all-reduce.3.cloned.1.call-done = (f32[1152,1152]{1,0:T(8,128)}, f32[1152,768]{1,0:T(8,128)}) async-done(((f32[1152,1152]{1,0:T(8,128)}, f32[1152,768]{1,0:T(8,128)}), (f32[1152,1152]{1,0:T(8,128)}, f32[1152,768]{1,0:T(8,128)})) %all-reduce.3.cloned.1.call-update) | async-done | bytes 8847376 | tf_op jit(solution)/shard_map/psum | solution.py:161
  192.2 234.7 %shard_map.30 = (f32[256,768]{1,0:T(8,128)}, f32[1152,768]{1,0:T(8,128)}) custom-call(f32[256,1152]{1,0:T(8,128)} %slice.8.p_ref, f32[256,768]{1,0:T(8,128)} %w_ref.1, f32[1152,1152]{1,0:T(8,128)} %get-tuple-element.2.m_ref, f32[1152,768]{1,0:T(8,128)} %get-tuple-element.3.g_ref), custom_call_target="tpu_custom_call" | custom-call | tf_op jit(solution)/shard_map/pallas_call | solution.py:165
Async XLA Ops:
  7.2 39.0 %copy-start.1 = (f32[256,768]{1,0:T(8,128)S(1)}, f32[256,768]{1,0:T(8,128)}, u32[]{:S(2)}) copy-start(f32[256,768]{1,0:T(8,128)} %w_ref.1) | copy-start | bytes 2359300
  7.2 39.0 %all-gather.2.cloned.1.call-start = ((), (), s32[]{:S(2)}) async-start(), calls=%async_computation | async-start | bytes 1966080 | tf_op jit(solution)/shard_map/all_gather | solution.py:160
  9.1 183.2 %all-reduce.3.cloned.1.call-start = ((), (), s32[]{:S(2)}) async-start(), calls=%async_computation.1 | async-start | bytes 17694720 | tf_op jit(solution)/shard_map/psum | solution.py:161
  46.2 6.2 %copy-start = (f32[256,1536]{1,0:T(8,128)S(1)}, f32[256,1536]{1,0:T(8,128)}, u32[]{:S(2)}) copy-start(f32[256,1536]{1,0:T(8,128)} %all-gather.2.cloned.1.call-done) | copy-start | bytes 4718596
Sparse Core Ops, SparseCore 0:
  10.1 36.0 all-gather.1
  59.7 132.4 all-reduce.2

commit v2 on v1

--- a/solution.py
+++ b/solution.py
@@ -101,7 +101,8 @@
         direct_inverse(x_ref, a_ref)
 
 
-def factor_kernel(root_rows, p_ref, w_ref, m_ref, g_ref, out_ref, fac_ref, q_ref, u_ref, c_ref, t_ref, x_ref):
+def factor_kernel(root_rows, p_ref, w_ref, v0_ref, v1_ref, v2_ref, out_ref, fac_ref, q_ref, u_ref, c_ref, t_ref, x_ref):
+    v_refs = (v0_ref, v1_ref, v2_ref)
     snap = lax.axis_index("snaps")
     n = PANEL
     row_ids, col_ids = grid_ids(n)
@@ -112,20 +113,21 @@
         return slice(k * n, (k + 1) * n)
 
     for k in range(PANELS):
-        acc = m_ref[blk(k), blk(k)]
+        acc = v_refs[k][:, :n]
         for j in range(k):
             acc = acc - dot6(u_ref[blk(j), blk(k)], u_ref[blk(j), blk(k)], ta=True)
         t_ref[...] = acc
         newton_inverse(x_ref, t_ref)
         x = x_ref[...]
         for i in range(k + 1, PANELS):
-            acc = m_ref[blk(k), blk(i)]
+            acc = v_refs[k][:, blk(i - k)]
             for j in range(k):
                 acc = acc - dot6(u_ref[blk(j), blk(k)], u_ref[blk(j), blk(i)], ta=True)
             u_ref[blk(k), blk(i)] = dot6(x, acc)
         for low, size in chunks:
             cols = slice(low, low + size)
-            acc = g_ref[blk(k), cols]
+            shift = (PANELS - k) * n
+            acc = v_refs[k][:, shift + low : shift + low + size]
             for j in range(k):
                 acc = acc - dot3(u_ref[blk(j), blk(k)], c_ref[blk(j), cols], ta=True)
             coeffs = dot3(x, acc)
@@ -152,15 +154,204 @@
             out_ref[:, :n] = q_ref[:, blk(k)] * root_rows
 
 
+def bit_order(n_bits, half):
+    return [0] + (list(range(1, n_bits)) if half == 0 else list(range(n_bits - 1, 0, -1)))
+
+
+def reduce_kernel(n_rows, n_snaps, w_ref, p_ref, o0_ref, o1_ref, o2_ref, *scratch):
+    v_refs, lands = scratch[:PANELS], scratch[PANELS:-5]
+    z_send, z_recv, own_sem, send_sems, recv_sems = scratch[-5:]
+    o_refs = (o0_ref, o1_ref, o2_ref)
+    n = PANEL
+    n_bits = n_rows.bit_length() - 1
+    row = lax.axis_index("rows")
+    snap = lax.axis_index("snaps")
+    bits = [(row // 2**b) % 2 for b in range(n_bits)]
+    mates = [row + (1 - 2 * bits[b]) * 2**b for b in range(n_bits)]
+    up, down = lax.rem(snap + 1, n_snaps), lax.rem(snap + n_snaps - 1, n_snaps)
+
+    barrier = pltpu.get_barrier_semaphore()
+    for mate in mates:
+        pl.semaphore_signal(barrier, inc=1, device_id={"rows": mate})
+    for mate in (up, down):
+        pl.semaphore_signal(barrier, inc=1, device_id={"snaps": mate})
+    pl.semaphore_wait(barrier, n_bits + 2)
+
+    def panel(k):
+        return p_ref.at[:, k * n : (k + 1) * n]
+
+    def relay(k, way):
+        return pltpu.make_async_remote_copy(
+            src_ref=panel(k),
+            dst_ref=panel(k),
+            send_sem=z_send.at[k, way],
+            recv_sem=z_recv.at[k],
+            device_id={"snaps": up if way else down},
+        )
+
+    def pass_on(k):
+        @pl.when((snap >= k) & (snap < n_snaps - 1))
+        def _():
+            relay(k, 1).start()
+
+        @pl.when((snap <= k) & (snap > 0))
+        def _():
+            relay(k, 0).start()
+
+    for k in range(PANELS):
+
+        @pl.when(snap == k)
+        def _():
+            own = pltpu.make_async_copy(w_ref.at[:, :n], panel(k), own_sem)
+            own.start()
+            own.wait()
+            pass_on(k)
+
+    order = list(range(PANELS - 1, -1, -1))
+
+    def halves(k):
+        width = v_refs[k].shape[1]
+        split = (width // 256 + k // 2) * 128
+        return ((0, split), (split, width - split))
+
+    def spans(half):
+        first, size, out = 0, n, []
+        for b in bit_order(n_bits, half):
+            size //= 2
+            out.append((b, size, first + bits[b] * size, first + (1 - bits[b]) * size))
+            first = first + bits[b] * size
+        return out
+
+    stages = [spans(0), spans(1)]
+
+    def window(refs, k, half, first, size):
+        low, width = halves(k)[half]
+        return refs[k].at[pl.ds(pl.multiple_of(first, 8), size), low : low + width]
+
+    def copy(k, half, step):
+        down_step = step >= n_bits
+        stage = 2 * n_bits - 1 - step if down_step else step
+        b, size, kept, given = stages[half][stage]
+        if down_step:
+            src = dst = window(o_refs, k, half, kept, size)
+        else:
+            src = window(v_refs, k, half, given, size)
+            dst = lands[(k * 2 + half) * n_bits + stage]
+        return pltpu.make_async_remote_copy(
+            src_ref=src,
+            dst_ref=dst,
+            send_sem=send_sems.at[k, half, step],
+            recv_sem=recv_sems.at[k, half, step],
+            device_id={"rows": mates[b]},
+        )
+
+    def finish(k, half, step):
+        copy(k, half, step).wait_recv()
+        if step < n_bits:
+            b, size, kept, given = stages[half][step]
+            view = window(v_refs, k, half, kept, size)
+            into = view if step < n_bits - 1 else window(o_refs, k, half, kept, size)
+            into[...] = view[...] + lands[(k * 2 + half) * n_bits + step][...]
+
+    def compute(k):
+        left = p_ref[:, k * n : (k + 1) * n]
+        for i in range(k, PANELS):
+            v_refs[k][:, (i - k) * n : (i - k + 1) * n] = dot6(
+                left, p_ref[:, i * n : (i + 1) * n], ta=True
+            )
+        shift = (PANELS - k) * n
+        for low in range(0, w_ref.shape[1], n):
+            v_refs[k][:, shift + low : shift + low + n] = dot6(
+                left, w_ref[:, low : low + n], ta=True
+            )
+
+    steps = 2 * n_bits
+    for tick in range(steps + PANELS):
+        for place, k in enumerate(order):
+            step = tick - place
+            if step == 0:
+
+                @pl.when(snap != k)
+                def _():
+                    relay(k, 0).wait_recv()
+                    pass_on(k)
+
+                compute(k)
+            for half in range(2):
+                if 1 <= step <= steps:
+                    finish(k, half, step - 1)
+                if 0 <= step < steps:
+                    copy(k, half, step).start()
+
+    for k in range(PANELS):
+        for half in range(2):
+            for step in range(steps):
+                copy(k, half, step).wait_send()
+
+        @pl.when((snap >= k) & (snap < n_snaps - 1))
+        def _():
+            relay(k, 1).wait_send()
+
+        @pl.when((snap <= k) & (snap > 0))
+        def _():
+            relay(k, 0).wait_send()
+
+
+def reduced_by_copies(snapshots, n_rows, n_snaps):
+    rows_dev, cols_dev = snapshots.shape
+    n_bits = n_rows.bit_length() - 1
+    widths = [(PANELS - k) * PANEL + cols_dev for k in range(PANELS)]
+    lands = []
+    for k, width in enumerate(widths):
+        split = (width // 256 + k // 2) * 128
+        for part in (split, width - split):
+            lands += [pltpu.VMEM((PANEL >> (s + 1), part), F32) for s in range(n_bits)]
+    vmem = pl.BlockSpec(memory_space=pltpu.VMEM)
+    dma = pltpu.SemaphoreType.DMA
+    return pl.pallas_call(
+        functools.partial(reduce_kernel, n_rows, n_snaps),
+        out_shape=[jax.ShapeDtypeStruct((rows_dev, PANELS * PANEL), F32)]
+        + [jax.ShapeDtypeStruct((PANEL, width), F32) for width in widths],
+        in_specs=[vmem],
+        out_specs=[vmem] * (1 + PANELS),
+        scratch_shapes=[pltpu.VMEM((PANEL, width), F32) for width in widths]
+        + lands
+        + [
+            dma((PANELS, 2)),
+            dma((PANELS,)),
+            dma(()),
+            dma((PANELS, 2, 2 * n_bits)),
+            dma((PANELS, 2, 2 * n_bits)),
+        ],
+        compiler_params=pltpu.CompilerParams(
+            collective_id=0, has_side_effects=True, vmem_limit_bytes=40 * 2**20
+        ),
+    )(snapshots)
+
+
+def reduced_by_collectives(snapshots):
+    total = PANEL * PANELS
+    panels = lax.all_gather(snapshots[:, :PANEL], "snaps", axis=1, tiled=True)[:, :total]
+    both = jnp.concatenate([panels, snapshots], axis=1)
+    sums = lax.psum(
+        [
+            dot6(panels[:, k * PANEL : (k + 1) * PANEL], both[:, k * PANEL :], ta=True)
+            for k in range(PANELS)
+        ],
+        "rows",
+    )
+    return [panels] + list(sums)
+
+
 def shards(snapshots):
     rows_dev, cols_dev = snapshots.shape
-    row_count = rows_dev * lax.axis_size("rows")
-    root_rows = float(row_count) ** 0.5
+    n_rows, n_snaps = lax.axis_size("rows"), lax.axis_size("snaps")
+    root_rows = float(rows_dev * n_rows) ** 0.5
     total = PANEL * PANELS
-    panels = lax.all_gather(snapshots[:, :PANEL], "snaps", axis=1, tiled=True)[:, :total]
-    gram, cross = lax.psum(
-        (dot6(panels, panels, ta=True), dot6(panels, snapshots, ta=True)), "rows"
-    )
+    if n_rows & (n_rows - 1) == 0 and PANEL % (8 * n_rows) == 0:
+        panels, *sums = reduced_by_copies(snapshots, n_rows, n_snaps)
+    else:
+        panels, *sums = reduced_by_collectives(snapshots)
     vmem = pl.BlockSpec(memory_space=pltpu.VMEM)
     return pl.pallas_call(
         functools.partial(factor_kernel, root_rows),
@@ -168,7 +359,7 @@
             jax.ShapeDtypeStruct((rows_dev, cols_dev), F32),
             jax.ShapeDtypeStruct((total, cols_dev), F32),
         ),
-        in_specs=[vmem] * 4,
+        in_specs=[vmem] * 5,
         out_specs=(vmem, vmem),
         scratch_shapes=[
             pltpu.VMEM((rows_dev, total), F32),
@@ -178,7 +369,7 @@
             pltpu.VMEM((PANEL, PANEL), F32),
         ],
         compiler_params=pltpu.CompilerParams(vmem_limit_bytes=56 * 2**20),
-    )(panels, snapshots, gram, cross)
+    )(panels, snapshots, *sums)
 
 
 def solution(mesh):

time: 443 us -> 344 us (0.78)
  waiting for transfers between devices: 169 us -> 0 us
  Pallas kernels: 235 us -> 330 us
  between operations: 14.5 us -> 1.1 us
  matrix products: 13.3 us -> 0 us
    psum x1 -> x0, waiting for transfers between devices: 132 us -> none  [shards(): lax.psum((dot6(panels, panels, ta=True), dot6(panels, snapshots, ta=True)...]
    pallas_call x0 -> x1, Pallas kernels: none -> 95.4 us  [reduced_by_copies(): pl.pallas_call(functools.partial(reduce_kernel, n_rows, n_snaps), out_sha...]
    all_gather x1 -> x0, waiting for transfers between devices: 37.1 us -> none  [shards(): lax.all_gather(snapshots[:, :PANEL], 'snaps', axis=1, tiled=True)[:, :total]]
    dot_general x2 -> x0, matrix products: 13.3 us -> none  [dot6(): lax.dot_general(a, b, dims(ta, tb), precision=lax.Precision.HIGHEST, pref...]
    unnamed x4 -> x10, local copies, waits for them, and re-layouts: 0.01 us -> 6.41 us
  transfers between devices with their start and end apart: 2 -> 0, of which waited for: 2 -> 0; matrix products, arithmetic and copies ran while one was open for 0% -> 0% of each run, Pallas kernels for 0% -> 0%
where the time goes in v2:
time: 344 us; the launch traced here: 337 us
  Pallas kernels  330 us (96%)
  local copies, waits for them, and re-layouts  6.41 us (2%)
    pallas_call x1, Pallas kernels, shards(): pl.pallas_call(functools.partial(factor_kernel, root_rows), out_shape=(ja...  234 us
    pallas_call x1, Pallas kernels, reduced_by_copies(): pl.pallas_call(functools.partial(reduce_kernel, n_rows, n_snaps), out_sha...  95.4 us

profile of v2, /device:TPU:27, one launch (start us, length us, event | category | flops | bytes accessed | tf_op | source)
XLA Modules:
  0.0 337.1 jit_solution(13353024021576274000)
XLA Ops:
  0.6 0.0 copy-start
  0.6 1.1 copy-done
  1.8 95.4 %shard_map.30 = (f32[256,1152]{1,0:T(8,128)S(1)}, f32[384,1920]{1,0:T(8,128)S(1)}, f32[384,1536]{1,0:T(8,128)S(1)}, f32[384,1152]{1,0:T(8,128)S(1)}) custom-call(f32[256,768]{1,0:T(8,128)S(1)} %copy-done), custom_call_target="tpu_custom_call" | custom-call | tf_op jit(solution)/shard_map/pallas_call | solution.py:311
  97.2 0.0 copy-start.1
  97.2 1.6 copy-done.1
  98.8 0.0 copy-start.2
  98.8 1.4 copy-done.2
  100.2 0.0 copy-start.3
  100.2 1.2 copy-done.3
  101.4 0.0 copy-start.4
  101.4 1.0 copy-done.4
  102.5 234.2 %shard_map.31 = (f32[256,768]{1,0:T(8,128)}, f32[1152,768]{1,0:T(8,128)}) custom-call(f32[256,1152]{1,0:T(8,128)} %copy-done.4, f32[256,768]{1,0:T(8,128)} %w_ref.3, f32[384,1920]{1,0:T(8,128)} %copy-done.1, f32[384,1536]{1,0:T(8,128)} %copy-done.2, f32[384,1152]{1,0:T(8,128)} %copy-done.3), custom_call_target="tpu_custom_call" | custom-call | tf_op jit(solution)/shard_map/pallas_call | solution.py:356
Async XLA Ops:
  0.6 1.1 copy-start
  97.2 1.6 copy-start.1
  98.8 1.4 copy-start.2
  100.2 1.2 copy-start.3
  101.4 1.0 copy-start.4
